TPU v7x, 256 devices: a whole 4x4x8 slice. The times are simulated.
256 devices in a mesh: region: 32 (over x, y, core), industry: 8 (over z).
Axes of the slice: x: 4, y: 4, z: 8, core: 2. Of those that a mesh axis runs over, the one named last changes fastest.
Arguments:
- position: bfloat16 [8, 1536, 16, 1024], P(None, 'region', None, 'industry'), may hold values from 0.049804688 to 0.94921875
- dual_lower: bfloat16 [8, 1536, 16, 1024], P(None, 'region', None, 'industry'), may hold values from 0.099609375 to 10
- dual_upper: bfloat16 [8, 1536, 16, 1024], P(None, 'region', None, 'industry'), may hold values from 0.099609375 to 10
- upper_bound: int32 [1536, 16, 1024], P('region', None, 'industry'), may hold values from 2 to 63
- suppressed: int32 [1536, 16, 1024], P('region', None, 'industry'), may hold values from 0 to 1
- attack_region: int32 [8], replicated, may hold values from 0 to 1535
- attack_column: int32 [8], replicated, may hold values from 0 to 16383
- dual_row: float32 [8, 1536, 16], P(None, 'region'), may hold values from -3 to 3
- dual_col: float32 [8, 16, 1024], P(None, None, 'industry'), may hold values from -3 to 3
Outputs:
- cell_step: bfloat16 [8, 1536, 16, 1024], P(None, 'region', None, 'industry')
- row_step: float32 [8, 1536, 16], P(None, 'region')
- col_step: float32 [8, 16, 1024], P(None, None, 'industry')
All inputs are finite; a program needn't handle non-finite values.
Results may differ from a plain program's by a relative error of at most 0.001.
Values sent between devices are 32-bit elements; how exact they have to be, the bound alone decides.
A program may use at most 64 MiB of HBM per device.

v0:
```python
import jax
import jax.numpy as jnp
from jax import lax
from jax.sharding import PartitionSpec as P

ITERS = 3


weight_attack = 8.0
barrier = 0.5
shift_diag = 1.0


def row_margin(partial_value):
    return lax.psum(partial_value, "industry")


def col_margin(partial_value):
    return lax.psum(partial_value, "region")


def couple(scaling, part_row, part_col):
    left = row_margin(jnp.sum(scaling * part_col[:, None, :, :], axis=3))
    right = col_margin(jnp.sum(scaling * part_row[..., None], axis=1))
    return (left, right)


def local_pair(first_row, second_row, first_col, second_col):
    row_flag = (lax.axis_index("industry") == 0).astype(jnp.float32)
    col_flag = (lax.axis_index("region") == 0).astype(jnp.float32)
    return row_flag * jnp.sum(first_row * second_row, axis=(1, 2)) + col_flag * jnp.sum(
        first_col * second_col, axis=(1, 2)
    )


def inner_pair(first_row, second_row, first_col, second_col):
    return lax.psum(
        local_pair(first_row, second_row, first_col, second_col), ("region", "industry")
    )


def local(
    position,
    dual_lower,
    dual_upper,
    upper_bound,
    suppressed,
    attack_region,
    attack_column,
    dual_row,
    dual_col,
):
    rows_local = upper_bound.shape[0]
    sizes_count = upper_bound.shape[1]
    inds_local = upper_bound.shape[2]
    inds_total = inds_local * lax.axis_size("industry")
    region_ids = lax.axis_index("region") * rows_local + jnp.arange(rows_local, dtype=jnp.int32)
    column_ids = (
        jnp.arange(sizes_count, dtype=jnp.int32)[:, None] * inds_total
        + lax.axis_index("industry") * inds_local
        + jnp.arange(inds_local, dtype=jnp.int32)[None, :]
    )
    attacked = (region_ids[None, :, None, None] == attack_region[:, None, None, None]) & (
        column_ids[None, None] == attack_column[:, None, None, None]
    )
    active = jnp.maximum(suppressed[None], attacked.astype(jnp.int32)).astype(jnp.float32)
    upper = upper_bound.astype(jnp.float32)[None]
    value = position.astype(jnp.float32) * upper
    slack = upper - value
    scaling = active / (
        dual_lower.astype(jnp.float32) / value + dual_upper.astype(jnp.float32) / slack
    )
    gradient = (
        jnp.where(attacked, jnp.float32(weight_attack), jnp.float32(0.0))
        - dual_row[..., None]
        - dual_col[:, None]
        + barrier * (1.0 / value - 1.0 / slack)
    )
    margin_term = active * (0.5 * upper - value) + scaling * gradient
    res_row, diag_row = row_margin((jnp.sum(margin_term, axis=3), jnp.sum(scaling, axis=3)))
    res_col, diag_col = col_margin((jnp.sum(margin_term, axis=1), jnp.sum(scaling, axis=1)))
    diag_row = diag_row + shift_diag
    diag_col = diag_col + shift_diag

    def precondition(vec_row, vec_col):
        base_row, base_col = (vec_row / diag_row, vec_col / diag_col)
        once_row, once_col = couple(scaling, base_row, base_col)
        once_row, once_col = (once_row / diag_row, once_col / diag_col)
        twice_row, twice_col = couple(scaling, once_row, once_col)
        twice_row, twice_col = (twice_row / diag_row, twice_col / diag_col)
        pre_row = base_row - once_row + twice_row
        pre_col = base_col - once_col + twice_col
        rz_value = inner_pair(vec_row, pre_row, vec_col, pre_col)
        return (pre_row, pre_col, rz_value)

    pre_row, pre_col, rz_now = precondition(res_row, res_col)
    dir_row, dir_col = (pre_row, pre_col)
    sol_row = jnp.zeros_like(res_row)
    sol_col = jnp.zeros_like(res_col)
    for iteration in range(ITERS):
        image_row, image_col = couple(scaling, dir_row, dir_col)
        image_row = diag_row * dir_row + image_row
        image_col = diag_col * dir_col + image_col
        curvature_sum = inner_pair(dir_row, image_row, dir_col, image_col)
        step_len = (rz_now / curvature_sum)[:, None, None]
        sol_row = sol_row + step_len * dir_row
        sol_col = sol_col + step_len * dir_col
        res_row = res_row - step_len * image_row
        res_col = res_col - step_len * image_col
        if iteration + 1 < ITERS:
            pre_row, pre_col, rz_next = precondition(res_row, res_col)
            step_ratio = (rz_next / rz_now)[:, None, None]
            dir_row = pre_row + step_ratio * dir_row
            dir_col = pre_col + step_ratio * dir_col
            rz_now = rz_next
    cell_step = (scaling * (sol_row[..., None] + sol_col[:, None] - gradient)).astype(jnp.bfloat16)
    return (cell_step, sol_row, sol_col)


def solution(mesh):
    placed = (
        P(None, "region", None, "industry"),
        P(None, "region", None, "industry"),
        P(None, "region", None, "industry"),
        P("region", None, "industry"),
        P("region", None, "industry"),
        P(),
        P(),
        P(None, "region", None),
        P(None, None, "industry"),
    )
    return jax.shard_map(
        local,
        mesh=mesh,
        in_specs=placed,
        out_specs=(
            P(None, "region", None, "industry"),
            P(None, "region", None),
            P(None, None, "industry"),
        ),
        check_vma=False,
    )
```

profile of v0, /device:TPU:1, one launch (start us, length us, event | category | flops | bytes accessed | tf_op | source)
XLA Modules:
  0.0 1710.0 jit_solution(12762155836494898792)
XLA Ops:
  7.2 1.8 convert_element_type.41
  9.0 1.8 broadcast_multiply_fusion
  13.3 5.4 fusion.22
  18.7 4.5 fusion.21
  23.3 32.9 %all-reduce.2 = (f32[8,48,16]{2,1,0:T(8,128)}, f32[8,48,16]{2,1,0:T(8,128)S(1)}) all-reduce(f32[8,48,16]{2,1,0:T(8,128)} %get-tuple-element.24, f32[8,48,16]{2,1,0:T(8,128)} %get-tuple-element.26), channel_id=1, replica_groups=mesh['region'=32,'industry'=8] {'industry'}, use_global_device_ids=true, to_apply=%region_1.2 | all-reduce | flops 12288 | bytes 98304 | tf_op jit(solution)/shard_map/psum | solution.py:15
  56.3 1.6 fusion.14
  57.9 79.6 %all-reduce.32.cloned.1.call-done = (f32[8,16,128]{2,1,0:T(8,128)}, f32[8,16,128]{2,1,0:T(8,128)}) async-done(((f32[8,16,128]{2,1,0:T(8,128)}, f32[8,16,128]{2,1,0:T(8,128)}), (f32[8,16,128]{2,1,0:T(8,128)}, f32[8,16,128]{2,1,0:T(8,128)})) %all-reduce.32.cloned.1.call-update) | async-done | bytes 131088 | tf_op jit(solution)/shard_map/psum | solution.py:19
  138.4 3.4 multiply_reduce_fusion.16
  141.9 26.6 %psum.200 = f32[8,48,16]{2,1,0:T(8,128)} all-reduce(f32[8,48,16]{2,1,0:T(8,128)} %get-tuple-element.23), channel_id=1, replica_groups=mesh['region'=32,'industry'=8] {'industry'}, use_global_device_ids=true, to_apply=%region_9.10 | all-reduce | flops 6144 | bytes 49152 | tf_op jit(solution)/shard_map/psum | solution.py:15
  168.5 1.6 fusion.13
  170.2 77.7 %all-reduce.14.cloned.1.call-done = f32[8,16,128]{2,1,0:T(8,128)} async-done(((f32[8,16,128]{2,1,0:T(8,128)}), f32[8,16,128]{2,1,0:T(8,128)}) %all-reduce.14.cloned.1.call-update) | async-done | bytes 65552 | tf_op jit(solution)/shard_map/psum | solution.py:19
  248.7 3.4 multiply_reduce_fusion.15
  252.2 26.7 %psum.202 = f32[8,48,16]{2,1,0:T(8,128)} all-reduce(f32[8,48,16]{2,1,0:T(8,128)} %get-tuple-element.20), channel_id=1, replica_groups=mesh['region'=32,'industry'=8] {'industry'}, use_global_device_ids=true, to_apply=%region_13.14 | all-reduce | flops 6144 | bytes 49152 | tf_op jit(solution)/shard_map/psum | solution.py:15
  278.9 1.8 divide_add_fusion.2
  280.8 107.0 %all-reduce.16.cloned.1.call-done = f32[8,16,128]{2,1,0:T(8,128)} async-done(((f32[8,16,128]{2,1,0:T(8,128)}), f32[8,16,128]{2,1,0:T(8,128)}) %all-reduce.16.cloned.1.call-update) | async-done | bytes 65552 | tf_op jit(solution)/shard_map/psum | solution.py:19
  388.7 3.4 multiply_reduce_fusion.13
  392.1 26.7 %psum.205 = f32[8,48,16]{2,1,0:T(8,128)} all-reduce(f32[8,48,16]{2,1,0:T(8,128)} %get-tuple-element.18), channel_id=1, replica_groups=mesh['region'=32,'industry'=8] {'industry'}, use_global_device_ids=true, to_apply=%region_20.21 | all-reduce | flops 6144 | bytes 49152 | tf_op jit(solution)/shard_map/psum | solution.py:15
  418.9 1.8 multiply_reduce_fusion.22
  420.7 107.1 %all-reduce.18.cloned.1.call-done = f32[8,16,128]{2,1,0:T(8,128)} async-done(((f32[8,16,128]{2,1,0:T(8,128)}), f32[8,16,128]{2,1,0:T(8,128)}) %all-reduce.18.cloned.1.call-update) | async-done | bytes 65552 | tf_op jit(solution)/shard_map/psum | solution.py:19
  527.8 1.0 multiply_reduce_fusion.28
  528.8 1.2 multiply_add_fusion.14
  530.0 75.1 %all-reduce = (f32[8]{0:T(128)}, f32[8]{0:T(128)}) all-reduce(f32[8]{0:T(128)} %get-tuple-element.56, f32[8]{0:T(128)} %get-tuple-element.55), channel_id=1, replica_groups=mesh['region'=32,'industry'=8] {'region','industry'}, use_global_device_ids=true, to_apply=%region_18.19 | all-reduce | flops 16 | bytes 128 | tf_op jit(solution)/shard_map/psum | solution.py:37
  605.7 1.9 fusion.12
  607.6 1.5 fusion.18
  609.2 2.5 multiply_reduce_fusion.10
  611.8 26.5 %psum.208 = f32[8,48,16]{2,1,0:T(8,128)} all-reduce(f32[8,48,16]{2,1,0:T(8,128)} %get-tuple-element.17), channel_id=1, replica_groups=mesh['region'=32,'industry'=8] {'industry'}, use_global_device_ids=true, to_apply=%region_27.28 | all-reduce | flops 6144 | bytes 49152 | tf_op jit(solution)/shard_map/psum | solution.py:15
  638.2 1.6 fusion.11
  639.9 74.5 %all-reduce.20.cloned.1.call-done = f32[8,16,128]{2,1,0:T(8,128)} async-done(((f32[8,16,128]{2,1,0:T(8,128)}), f32[8,16,128]{2,1,0:T(8,128)}) %all-reduce.20.cloned.1.call-update) | async-done | bytes 65552 | tf_op jit(solution)/shard_map/psum | solution.py:19
  715.2 3.4 multiply_reduce_fusion.9
  718.6 26.7 %psum.210 = f32[8,48,16]{2,1,0:T(8,128)} all-reduce(f32[8,48,16]{2,1,0:T(8,128)} %get-tuple-element.14), channel_id=1, replica_groups=mesh['region'=32,'industry'=8] {'industry'}, use_global_device_ids=true, to_apply=%region_31.32 | all-reduce | flops 6144 | bytes 49152 | tf_op jit(solution)/shard_map/psum | solution.py:15
  745.4 2.5 multiply_reduce_fusion.21
  747.9 106.5 %all-reduce.22.cloned.1.call-done = f32[8,16,128]{2,1,0:T(8,128)} async-done(((f32[8,16,128]{2,1,0:T(8,128)}), f32[8,16,128]{2,1,0:T(8,128)}) %all-reduce.22.cloned.1.call-update) | async-done | bytes 65552 | tf_op jit(solution)/shard_map/psum | solution.py:19
  854.3 1.5 multiply_reduce_fusion.27
  856.5 75.2 %psum.212 = f32[8]{0:T(128)S(1)} all-reduce(f32[8]{0:T(128)S(1)} %multiply_add_fusion.13), channel_id=1, replica_groups=mesh['region'=32,'industry'=8] {'region','industry'}, use_global_device_ids=true, to_apply=%region_36.37 | all-reduce | flops 8 | bytes 64 | tf_op jit(solution)/shard_map/psum | solution.py:37
  933.3 1.1 multiply_add_fusion.3
  935.1 2.5 multiply_reduce_fusion.7
  937.6 25.1 %psum.213 = f32[8,48,16]{2,1,0:T(8,128)} all-reduce(f32[8,48,16]{2,1,0:T(8,128)} %get-tuple-element.12), channel_id=1, replica_groups=mesh['region'=32,'industry'=8] {'industry'}, use_global_device_ids=true, to_apply=%region_38.39 | all-reduce | flops 6144 | bytes 49152 | tf_op jit(solution)/shard_map/psum | solution.py:15
  962.7 1.7 multiply_reduce_fusion.20
  964.4 107.2 %all-reduce.24.cloned.1.call-done = f32[8,16,128]{2,1,0:T(8,128)} async-done(((f32[8,16,128]{2,1,0:T(8,128)}), f32[8,16,128]{2,1,0:T(8,128)}) %all-reduce.24.cloned.1.call-update) | async-done | bytes 65552 | tf_op jit(solution)/shard_map/psum | solution.py:19
  1071.7 1.0 multiply_reduce_fusion.26
  1072.6 1.1 multiply_add_fusion.12
  1073.8 75.0 %psum.215 = f32[8]{0:T(128)} all-reduce(f32[8]{0:T(128)} %multiply_add_fusion.12), channel_id=1, replica_groups=mesh['region'=32,'industry'=8] {'region','industry'}, use_global_device_ids=true, to_apply=%region_43.44 | all-reduce | flops 8 | bytes 64 | tf_op jit(solution)/shard_map/psum | solution.py:37
  1149.5 1.9 fusion.10
  1151.3 1.6 fusion.16
  1152.9 2.5 multiply_reduce_fusion.4
  1155.5 26.3 %psum.216 = f32[8,48,16]{2,1,0:T(8,128)} all-reduce(f32[8,48,16]{2,1,0:T(8,128)} %get-tuple-element.11), channel_id=1, replica_groups=mesh['region'=32,'industry'=8] {'industry'}, use_global_device_ids=true, to_apply=%region_45.46 | all-reduce | flops 6144 | bytes 49152 | tf_op jit(solution)/shard_map/psum | solution.py:15
  1181.9 1.6 fusion.9
  1183.5 74.7 %all-reduce.26.cloned.1.call-done = f32[8,16,128]{2,1,0:T(8,128)} async-done(((f32[8,16,128]{2,1,0:T(8,128)}), f32[8,16,128]{2,1,0:T(8,128)}) %all-reduce.26.cloned.1.call-update) | async-done | bytes 65552 | tf_op jit(solution)/shard_map/psum | solution.py:19
  1259.1 3.4 multiply_reduce_fusion.3
  1262.5 26.7 %psum.218 = f32[8,48,16]{2,1,0:T(8,128)} all-reduce(f32[8,48,16]{2,1,0:T(8,128)} %get-tuple-element.8), channel_id=1, replica_groups=mesh['region'=32,'industry'=8] {'industry'}, use_global_device_ids=true, to_apply=%region_49.50 | all-reduce | flops 6144 | bytes 49152 | tf_op jit(solution)/shard_map/psum | solution.py:15
  1289.3 2.4 multiply_reduce_fusion.19
  1291.7 106.5 %all-reduce.28.cloned.1.call-done = f32[8,16,128]{2,1,0:T(8,128)} async-done(((f32[8,16,128]{2,1,0:T(8,128)}), f32[8,16,128]{2,1,0:T(8,128)}) %all-reduce.28.cloned.1.call-update) | async-done | bytes 65552 | tf_op jit(solution)/shard_map/psum | solution.py:19
  1398.2 1.6 multiply_reduce_fusion.25
  1399.7 1.1 multiply_add_fusion.11
  1400.8 75.0 %psum.220 = f32[8]{0:T(128)} all-reduce(f32[8]{0:T(128)} %multiply_add_fusion.11), channel_id=1, replica_groups=mesh['region'=32,'industry'=8] {'region','industry'}, use_global_device_ids=true, to_apply=%region_54.55 | all-reduce | flops 8 | bytes 64 | tf_op jit(solution)/shard_map/psum | solution.py:37
  1477.5 1.1 multiply_add_fusion.1
  1479.3 2.5 multiply_reduce_fusion.1
  1481.8 25.0 %psum.221 = f32[8,48,16]{2,1,0:T(8,128)} all-reduce(f32[8,48,16]{2,1,0:T(8,128)} %get-tuple-element.6), channel_id=1, replica_groups=mesh['region'=32,'industry'=8] {'industry'}, use_global_device_ids=true, to_apply=%region_56.57 | all-reduce | flops 6144 | bytes 49152 | tf_op jit(solution)/shard_map/psum | solution.py:15
  1506.9 1.7 multiply_reduce_fusion.18
  1508.6 107.5 %all-reduce.30.cloned.1.call-done = f32[8,16,128]{2,1,0:T(8,128)} async-done(((f32[8,16,128]{2,1,0:T(8,128)}), f32[8,16,128]{2,1,0:T(8,128)}) %all-reduce.30.cloned.1.call-update) | async-done | bytes 65552 | tf_op jit(solution)/shard_map/psum | solution.py:19
  1616.0 1.0 multiply_reduce_fusion.24
  1617.6 75.0 %psum.223 = f32[8]{0:T(128)S(1)} all-reduce(f32[8]{0:T(128)S(1)} %multiply_add_fusion.10), channel_id=1, replica_groups=mesh['region'=32,'industry'=8] {'region','industry'}, use_global_device_ids=true, to_apply=%region_61.62 | all-reduce | flops 8 | bytes 64 | tf_op jit(solution)/shard_map/psum | solution.py:37
  1693.3 1.2 multiply_add_fusion
  1696.2 6.9 multiply_convert_fusion
  (76 shorter events, 17.0 us)
Async XLA Ops:
  7.2 130.3 %all-reduce.32.cloned.1.call-start = ((), (), s32[]{:S(2)}) async-start(), calls=%async_computation.9 | async-start | bytes 262144 | tf_op jit(solution)/shard_map/psum | solution.py:19
  11.8 6.9 copy-start.5
  12.5 6.2 copy-start.13
  13.3 5.4 copy-start
  13.3 5.4 copy-start.3
  13.3 5.4 copy-start.6
  13.3 5.4 copy-start.7
  13.3 5.4 copy-start.11
  23.3 224.6 %all-reduce.14.cloned.1.call-start = ((), (), s32[]{:S(2)}) async-start(), calls=%async_computation | async-start | bytes 131072 | tf_op jit(solution)/shard_map/psum | solution.py:19
  137.5 110.4 %copy-start.1 = (f32[8,16,128]{2,1,0:T(8,128)S(1)}, f32[8,16,128]{2,1,0:T(8,128)}, u32[]{:S(2)}) copy-start(f32[8,16,128]{2,1,0:T(8,128)} %get-tuple-element.35) | copy-start | bytes 196612
  141.8 246.0 %all-reduce.16.cloned.1.call-start = ((), (), s32[]{:S(2)}) async-start(), calls=%async_computation.1 | async-start | bytes 131072 | tf_op jit(solution)/shard_map/psum | solution.py:19
  141.9 245.9 %copy-start.9 = (f32[8,16,128]{2,1,0:T(8,128)S(1)}, f32[8,16,128]{2,1,0:T(8,128)}, u32[]{:S(2)}) copy-start(f32[8,16,128]{2,1,0:T(8,128)} %get-tuple-element.34) | copy-start | bytes 196612
  278.9 248.9 %all-reduce.18.cloned.1.call-start = ((), (), s32[]{:S(2)}) async-start(), calls=%async_computation.2 | async-start | bytes 131072 | tf_op jit(solution)/shard_map/psum | solution.py:19
  418.9 295.5 %all-reduce.20.cloned.1.call-start = ((), (), s32[]{:S(2)}) async-start(), calls=%async_computation.3 | async-start | bytes 131072 | tf_op jit(solution)/shard_map/psum | solution.py:19
  605.7 3.4 copy-start.14
  611.7 242.6 %all-reduce.22.cloned.1.call-start = ((), (), s32[]{:S(2)}) async-start(), calls=%async_computation.4 | async-start | bytes 131072 | tf_op jit(solution)/shard_map/psum | solution.py:19
  611.8 242.5 %copy-start.10 = (f32[8,16,128]{2,1,0:T(8,128)S(1)}, f32[8,16,128]{2,1,0:T(8,128)}, u32[]{:S(2)}) copy-start(f32[8,16,128]{2,1,0:T(8,128)} %get-tuple-element.51) | copy-start | bytes 196612
  745.4 326.3 %all-reduce.24.cloned.1.call-start = ((), (), s32[]{:S(2)}) async-start(), calls=%async_computation.5 | async-start | bytes 131072 | tf_op jit(solution)/shard_map/psum | solution.py:19
  931.7 0.6 copy-start.16
  934.4 0.7 copy-start.2
  962.7 295.5 %all-reduce.26.cloned.1.call-start = ((), (), s32[]{:S(2)}) async-start(), calls=%async_computation.6 | async-start | bytes 131072 | tf_op jit(solution)/shard_map/psum | solution.py:19
  1149.4 1.9 copy-start.15
  1155.5 242.7 %all-reduce.28.cloned.1.call-start = ((), (), s32[]{:S(2)}) async-start(), calls=%async_computation.7 | async-start | bytes 131072 | tf_op jit(solution)/shard_map/psum | solution.py:19
  1289.2 326.8 %all-reduce.30.cloned.1.call-start = ((), (), s32[]{:S(2)}) async-start(), calls=%async_computation.8 | async-start | bytes 131072 | tf_op jit(solution)/shard_map/psum | solution.py:19
  1477.5 4.4 copy-start.8
  1478.6 0.7 copy-start.4
  1695.5 7.7 copy-start.12
Sparse Core Ops, SparseCore 0:
  23.4 114.0 all-reduce.31
  142.0 105.8 all-reduce.13
  279.0 108.7 all-reduce.15
  419.0 108.7 all-reduce.17
  611.9 102.4 all-reduce.19
  745.5 108.7 all-reduce.21
  962.8 108.8 all-reduce.23
  1155.6 102.5 all-reduce.25
  1289.4 108.7 all-reduce.27
  1507.0 108.9 all-reduce.29
where the time goes:
time: 1710 us
  waiting for transfers between devices  948 us (55%)
  blocking collectives  645 us (38%)
  other arithmetic  99.3 us (6%)
    psum x10, waiting for transfers between devices, col_margin(): return lax.psum(partial_value, 'region')  948 us
    psum x5, blocking collectives, inner_pair(): lax.psum(local_pair(first_row, second_row, first_col, second_col), ('regi...  375 us
    psum x10, blocking collectives, row_margin(): return lax.psum(partial_value, 'industry')  269 us
  transfers between devices with their start and end apart: 10, of which 10 were waited for; matrix products, arithmetic and copies ran while one was open for 1% of the time, Pallas kernels for 0%

commit v1 on v0

v1 whole, which is shorter than its diff:
```python
import jax
import jax.numpy as jnp
from jax import lax
from jax.experimental import pallas as pl
from jax.experimental.pallas import tpu as pltpu
from jax.sharding import PartitionSpec as P

MESH = pl.DeviceIdType.MESH
F32 = jnp.float32
BF16 = jnp.bfloat16
K, RL, S, IL = 8, 48, 16, 128
KO = 4
NZ, NX, NY = 8, 4, 4
ROUNDS = 8
WEIGHT_ATTACK, BARRIER, SHIFT = 8.0, 0.5, 1.0
Z_STEPS = (4, 3, 5, 2, 6, 1, 7)
LINE_STEPS = (2, 1, 3)


def split_pair(x):
    high = x.astype(BF16)
    low = (x - high.astype(F32)).astype(BF16)
    return high, low


def split_three(x):
    high = x.astype(BF16)
    rest = x - high.astype(F32)
    mid = rest.astype(BF16)
    low = (rest - mid.astype(F32)).astype(BF16)
    return jnp.concatenate([high, mid, low], axis=0)


def pack(rows):
    tiles = [rows[q][8 * h : 8 * h + 8] for q in range(KO) for h in range(2)]
    lane = lax.broadcasted_iota(jnp.int32, (8, 128), 1)
    packed = []
    for i in range(6):
        spare = pltpu.roll(tiles[6 + i // 3], 96 - 32 * (i % 3), 1)
        packed.append(jnp.where(lane < 96, tiles[i], spare))
    return jnp.concatenate(packed, axis=0)


def unpack(packed):
    lane = lax.broadcasted_iota(jnp.int32, (8, 128), 1)
    zero = jnp.zeros((8, 128), F32)
    m = [packed[8 * i : 8 * i + 8] for i in range(6)]
    tiles = [jnp.where(lane < 96, x, zero) for x in m]
    for g in range(2):
        a = pltpu.roll(m[3 * g], 32, 1)
        b = pltpu.roll(m[3 * g + 1], 64, 1)
        c = pltpu.roll(m[3 * g + 2], 96, 1)
        tiles.append(
            jnp.where(lane < 32, a, jnp.where(lane < 64, b, jnp.where(lane < 96, c, zero)))
        )
    return [jnp.concatenate([tiles[2 * q], tiles[2 * q + 1]], axis=0) for q in range(KO)]


def kernel(
    pos_hbm, low_hbm, high_hbm, upper_hbm, supp_hbm, att_r, att_c, drow_hbm, dcol_hbm,
    cell_hbm, row_out, col_out,
    pos, low, high, upper, supp, drow, dcol, in_sem, small_sem,
    scal, scal_x, grad, drow_b, umat, amat, hmat, key, part, part_x, pair_s, pair_r,
    mat_c, mat_r,
    ini_zs, ini_zr, ini_c1, ini_c1r, ini_c2, ini_c2r, ini_s, ini_r,
    zs, zr, z_ss, z_rs,
    c1, c1r, c2, c2r, c_ss, c_rs,
    dzs, dzr, dps, dpr, d_ss, d_rs,
    hist_r, hist_c, dia_r, dia_c, inv_r, inv_c, vec_r, vec_c, cur_r, cur_c, scl,
    fin, fin_x, fin_r, cell, out_sem,
):
    reg = lax.axis_index("region")
    iz = lax.axis_index("industry")
    core = lax.rem(reg, 2)
    iy = lax.rem(reg // 2, NY)
    ix = reg // (2 * NY)
    kb = core * KO
    ks = KO - kb
    sibling = {"region": reg + 1 - 2 * core}

    def plane(x, y):
        return {"region": (x * NY + y) * 2 + core}

    x_peers = [plane(lax.rem(ix + h, NX), iy) for h in LINE_STEPS]
    y_peers = [plane(ix, lax.rem(iy + h, NY)) for h in LINE_STEPS]
    z_peers = [{"industry": lax.rem(iz + h, NZ)} for h in Z_STEPS]
    p_peers = [
        plane(lax.rem(ix + h, NX), lax.rem(iy + g, NY))
        for h in (2, 1, 3, 0)
        for g in (2, 1, 3, 0)
        if h or g
    ]
    everyone = [sibling] + z_peers + p_peers

    barrier = pltpu.get_barrier_semaphore()
    for peer in everyone:
        pl.semaphore_signal(barrier, inc=1, device_id=peer, device_id_type=MESH)

    def remote(src, dst, ss, rs, peer):
        return pltpu.make_async_remote_copy(
            src_ref=src, dst_ref=dst, send_sem=ss, recv_sem=rs, device_id=peer, device_id_type=MESH
        )

    def in_copies(k):
        return [
            pltpu.make_async_copy(a.at[k], b.at[k], in_sem.at[i, k])
            for i, (a, b) in enumerate(((pos_hbm, pos), (low_hbm, low), (high_hbm, high)))
        ]

    small = [
        pltpu.make_async_copy(a, b, small_sem.at[i])
        for i, (a, b) in enumerate(
            ((drow_hbm, drow), (dcol_hbm, dcol), (upper_hbm, upper), (supp_hbm, supp))
        )
    ]
    for c in small:
        c.start()
    for j in range(K):
        for c in in_copies(lax.rem(ks + j, K)):
            c.start()

    for c in small:
        c.wait()

    column = (
        lax.broadcasted_iota(jnp.int32, (S, IL), 0) * (NZ * IL)
        + iz * IL
        + lax.broadcasted_iota(jnp.int32, (S, IL), 1)
    )
    for k in range(K):
        key[k] = jnp.where(column == att_c[k], att_r[k] - reg * RL, -1)

    @pl.loop(0, K)
    def _(k):
        d = drow[k]
        for r in range(RL):
            drow_b[k, pl.ds(r * S, S), :] = jnp.broadcast_to(d[:, r : r + 1], (S, IL))

    @pl.loop(0, RL)
    def _(r):
        u = upper[r].astype(F32)
        umat[r] = u
        amat[r] = supp[r].astype(F32)
        hmat[r] = BARRIER / u

    lane = lax.broadcasted_iota(jnp.int32, (S, IL), 1)

    @pl.loop(0, K)
    def _(j):
        k = lax.rem(ks + j, K)
        for c in in_copies(k):
            c.wait()
        zero = jnp.zeros((S, IL), F32)
        dc = dcol[k]
        ky = key[k]

        def body(b, carry):
            row_s, row_m, col_s, col_m = carry
            for i in range(2):
                r = b * 2 + i
                rows = pl.ds(pl.multiple_of(r * S, S), S)
                p = pos[k, r].astype(F32)
                dl = low[k, r].astype(F32)
                du = high[k, r].astype(F32)
                u = umat[r]
                hit = ky == r
                act = jnp.where(hit, 1.0, amat[r])
                om = 1.0 - p
                q = p * om
                den = dl * om + du * p
                rc = 1.0 / (q * den)
                qr = q * rc
                au = act * u
                high_s, low_s = split_pair(au * q * qr)
                sc = high_s.astype(F32) + low_s.astype(F32)
                g = hmat[r] * (om - p) * (den * rc) + jnp.where(hit, WEIGHT_ATTACK, 0.0) - dc
                m = au * (0.5 - p) + sc * (g - drow_b[k, rows, :])
                scal[k, rows, :] = sc
                grad[k, rows, :] = g
                col_s = col_s + sc
                col_m = col_m + m
                row_s = jnp.where(lane == r, jnp.sum(sc, axis=1, keepdims=True), row_s)
                row_m = jnp.where(lane == r, jnp.sum(m, axis=1, keepdims=True), row_m)
            return row_s, row_m, col_s, col_m

        row_s, row_m, col_s, col_m = lax.fori_loop(0, RL // 2, body, (zero, zero, zero, zero))
        part[k, 0] = row_s
        part[k, 1] = row_m
        part[k, 2] = col_s
        part[k, 3] = col_m

    pl.semaphore_wait(barrier, len(everyone))

    pair_part = remote(part.at[pl.ds(ks, KO)], part_x, pair_s.at[0], pair_r.at[0], sibling)
    pair_scal = remote(scal.at[pl.ds(ks, KO)], scal_x, pair_s.at[1], pair_r.at[1], sibling)
    pair_part.start()
    pair_scal.start()
    pair_part.wait()

    row_s = [part[kb + q, 0] + pltpu.roll(part_x[q, 0], RL, 1) for q in range(KO)]
    row_m = [part[kb + q, 1] + pltpu.roll(part_x[q, 1], RL, 1) for q in range(KO)]
    for q in range(KO):
        for i in range(2):
            ini_c1[q // 2, pl.ds(((q % 2) * 2 + i) * S, S), :] = part[kb + q, 2 + i] + part_x[q, 2 + i]
    packed_s, packed_m = pack(row_s), pack(row_m)
    ini_zs[0:48, :] = packed_s
    ini_zs[48:96, :] = packed_m

    def line_start(src, dst, ss, rs, first_x):
        for h in range(3):
            for half in range(2):
                along_x = (half == 0) == first_x
                peer = (x_peers if along_x else y_peers)[h]
                slot = ix if along_x else iy
                remote(src.at[half], dst.at[half, slot], ss.at[half], rs.at[half], peer).start()

    def line_finish(src, dst, ss, rs, first_x):
        for half in range(2):
            along_x = (half == 0) == first_x
            slot = ix if along_x else iy
            dst[half, slot] = src[half]
        for half in range(2):
            got = dst.at[half, pl.ds(0, 3)]
            c = remote(got, got, ss.at[half], rs.at[half], x_peers[0])
            c.wait_recv()
            c.wait_send()
        return [dst[half, 0] + dst[half, 1] + dst[half, 2] + dst[half, 3] for half in range(2)]

    def z_start(src, dst, ss, rs):
        for peer in z_peers:
            remote(src, dst.at[iz], ss, rs, peer).start()

    def z_finish(src, dst, ss, rs):
        dst[iz] = src[...]
        got = dst.at[pl.ds(0, NZ - 1)]
        c = remote(got, got, ss, rs, z_peers[0])
        c.wait_recv()
        c.wait_send()
        t = [dst[i] for i in range(NZ)]
        return ((t[0] + t[1]) + (t[2] + t[3])) + ((t[4] + t[5]) + (t[6] + t[7]))

    z_start(ini_zs, ini_zr, ini_s.at[0], ini_r.at[0])
    line_start(ini_c1, ini_c1r, ini_s.at[pl.ds(1, 2)], ini_r.at[pl.ds(1, 2)], True)

    pair_scal.wait()

    def build(t):
        q, s = t // S, lax.rem(t, S)
        own = scal[kb + q, pl.ds(s, RL, stride=S), :]
        other = scal_x[q, pl.ds(s, RL, stride=S), :]
        both = jnp.concatenate([own, other], axis=0)
        h, l = split_pair(both)
        mat_c[q, s, :, 0:IL] = h
        mat_c[q, s, :, IL : 2 * IL] = l
        turned = jnp.transpose(jnp.concatenate([both, jnp.zeros((32, IL), F32)], axis=0))
        h, l = split_pair(turned)
        mat_r[q, s, :, 0:128] = h
        mat_r[q, s, :, 128:256] = l

    HALF_BUILD = KO * S // 2
    pl.loop(0, HALF_BUILD)(build)

    halves = line_finish(ini_c1, ini_c1r, ini_s.at[pl.ds(1, 2)], ini_r.at[pl.ds(1, 2)], True)
    for half in range(2):
        ini_c2[half] = halves[half]
    line_start(ini_c2, ini_c2r, ini_s.at[pl.ds(3, 2)], ini_r.at[pl.ds(3, 2)], False)

    pl.loop(HALF_BUILD, KO * S)(build)

    total = z_finish(ini_zs, ini_zr, ini_s.at[0], ini_r.at[0])
    used = lane < 2 * RL
    for q, (d, m) in enumerate(zip(unpack(total[0:48]), unpack(total[48:96]))):
        d = d + SHIFT
        inv = jnp.where(used, 1.0 / d, 0.0)
        dia_r[q] = d
        inv_r[q] = inv
        hist_r[0, q] = m * inv
        cur_r[q] = m * inv
    halves = line_finish(ini_c2, ini_c2r, ini_s.at[pl.ds(3, 2)], ini_r.at[pl.ds(3, 2)], False)
    for q in range(KO):
        at = (q % 2) * 2 * S
        d = halves[q // 2][at : at + S] + SHIFT
        m = halves[q // 2][at + S : at + 2 * S]
        inv = 1.0 / d
        dia_c[q] = d
        inv_c[q] = inv
        hist_c[0, q] = m * inv
        cur_c[q] = m * inv

    size_of = lax.rem(lax.broadcasted_iota(jnp.int32, (3 * S, 256), 0), S)

    def couple_half(mat, vec, q, depth):
        left = split_three(vec)[:, 0:depth]
        acc = jnp.zeros((3 * S, 256), F32)
        for s in range(S):
            prod = lax.dot_general(
                left, mat[q, s], (((1,), (0,)), ((), ())), preferred_element_type=F32
            )
            acc = jnp.where(size_of == s, prod, acc)
        acc = acc[0:S] + acc[S : 2 * S] + acc[2 * S : 3 * S]
        return acc[:, 0:128] + acc[:, 128:256]

    sub8 = lax.broadcasted_iota(jnp.int32, (8, 128), 0)
    lane8 = lax.broadcasted_iota(jnp.int32, (8, 128), 1)

    def dot_tile(products):
        tile = jnp.zeros((8, 128), F32)
        for d, per in enumerate(products):
            for q in range(KO):
                t = jnp.sum(jnp.sum(per[q], axis=0, keepdims=True), axis=1, keepdims=True)
                tile = jnp.where((sub8 == q) & (lane8 == d), jnp.broadcast_to(t, (8, 128)), tile)
        return tile

    def p_start(n, tile):
        dps[n] = tile
        for peer in p_peers:
            remote(dps.at[n], dpr.at[n, ix * NY + iy], d_ss.at[n], d_rs.at[n], peer).start()

    def p_finish(n):
        dpr[n, ix * NY + iy] = dps[n]
        got = dpr.at[n, pl.ds(0, NX * NY - 1)]
        c = remote(got, got, d_ss.at[n], d_rs.at[n], p_peers[0])
        c.wait_recv()
        c.wait_send()
        t = [dpr[n, i] for i in range(NX * NY)]
        while len(t) > 1:
            t = [t[i] + t[i + 1] for i in range(0, len(t), 2)]
        return t[0]

    def zd_start(n, tile):
        dzs[n] = tile
        z_start(dzs.at[n], dzr.at[n], d_ss.at[3 + n], d_rs.at[3 + n])

    def zd_finish(n):
        return z_finish(dzs.at[n], dzr.at[n], d_ss.at[3 + n], d_rs.at[3 + n])

    def value(n, q, d):
        return scl[n, q : q + 1, d : d + 1]

    def first_step(hist, vec, cur):
        for q in range(KO):
            alpha = value(0, q, 0) / value(0, q, 1)
            z0, w1, w3 = vec[0, q], hist[3, q], hist[5, q]
            z1 = z0 - alpha * (z0 + w3)
            vec[1, q] = z1
            vec[2, q] = hist[0, q] - alpha * (z0 + w1)
            vec[3, q] = alpha * z0
            cur[q] = z1

    def after_round(j, hist, vec, cur, dia, start):
        @pl.when((j != 2) & (j != 5))
        def _():
            for q in range(KO):
                cur[q] = hist[j, q]

        @pl.when(j == 2)
        def _():
            for q in range(KO):
                z0 = hist[0, q] - hist[1, q] + hist[2, q]
                vec[0, q] = z0
                cur[q] = z0

        @pl.when(j == 3)
        def _():
            rz, cv = [], []
            for q in range(KO):
                z0 = vec[0, q]
                dz = dia[q] * z0
                rz.append(dz * hist[0, q])
                cv.append(dz * (z0 + hist[3, q]))
            start(0, dot_tile([rz, cv]))

        @pl.when(j == 6)
        def _():
            rz, zn, zp = [], [], []
            for q in range(KO):
                z1 = vec[1, q]
                dz = dia[q] * z1
                rz.append(dz * vec[2, q])
                zn.append(dz * (z1 + hist[6, q]))
                zp.append(dz * (vec[0, q] + hist[3, q]))
            start(1, dot_tile([rz, zn, zp]))

    @pl.loop(0, ROUNDS + 1)
    def _(j):
        now = lax.rem(j, 2)
        nxt = 1 - now

        def lines(n):
            at = pl.ds(n * 2, 2)
            return (
                (c1.at[n], c1r.at[n], c_ss.at[0, at], c_rs.at[0, at], True),
                (c2.at[n], c2r.at[n], c_ss.at[1, at], c_rs.at[1, at], False),
            )

        @pl.when(j > 0)
        def _():
            first, second = lines(now)
            halves = line_finish(*first)
            for half in range(2):
                c2[now, half] = halves[half]
            line_start(*second)
            total = z_finish(zs.at[now], zr.at[now], z_ss.at[now], z_rs.at[now])
            for q, t in enumerate(unpack(total)):
                hist_r[j, q] = t * inv_r[q]

            @pl.when(j == 5)
            def _():
                scl[0] = zd_finish(0) + p_finish(0)
                first_step(hist_r, vec_r, cur_r)

            after_round(j, hist_r, vec_r, cur_r, dia_r, p_start)

        @pl.when(j < ROUNDS)
        def _():
            for q in range(KO):
                c1[nxt, q // 2, (q % 2) * S : (q % 2 + 1) * S, :] = couple_half(mat_c, cur_r[q], q, 96)
            line_start(*lines(nxt)[0])

        @pl.when(j > 0)
        def _():
            halves = line_finish(*lines(now)[1])
            for q in range(KO):
                at = (q % 2) * S
                hist_c[j, q] = halves[q // 2][at : at + S] * inv_c[q]

            @pl.when(j == 5)
            def _():
                first_step(hist_c, vec_c, cur_c)

            after_round(j, hist_c, vec_c, cur_c, dia_c, zd_start)

        @pl.when(j < ROUNDS)
        def _():
            zs[nxt] = pack([couple_half(mat_r, cur_c[q], q, 128) for q in range(KO)])
            z_start(zs.at[nxt], zr.at[nxt], z_ss.at[nxt], z_rs.at[nxt])

    scl[1] = zd_finish(1) + p_finish(1)
    steps = []
    for q in range(KO):
        beta = value(1, q, 0) / value(0, q, 0)
        curv = value(1, q, 1) + 2.0 * beta * value(1, q, 2) + beta * beta * value(0, q, 1)
        steps.append((beta, curv, value(1, q, 0) / curv))

    def second_step(hist, vec, cur, dia):
        rz, zp, zz = [], [], []
        for q in range(KO):
            beta, _, alpha = steps[q]
            p1 = vec[1, q] + beta * vec[0, q]
            np1 = p1 + hist[6, q] + beta * hist[3, q]
            z2 = vec[1, q] - alpha * (p1 + hist[8, q] + beta * hist[5, q])
            g2 = vec[2, q] - alpha * np1
            vec[3, q] = vec[3, q] + alpha * p1
            vec[4, q] = p1
            cur[q] = z2
            dz = dia[q] * z2
            rz.append(dz * g2)
            zp.append(dz * np1)
            zz.append(dz * z2)
        return [rz, zp, zz]

    dots_c = second_step(hist_c, vec_c, cur_c, dia_c)
    dots_r = second_step(hist_r, vec_r, cur_r, dia_r)
    cross = [2.0 * couple_half(mat_c, cur_r[q], q, 96) * cur_c[q] for q in range(KO)]
    zd_start(2, dot_tile(dots_c + [cross]))
    tile_r = dot_tile(dots_r)
    tile_c = zd_finish(2)
    p_start(2, tile_r + jnp.where(lane8 == 3, tile_c, 0.0))
    scl[2] = p_finish(2) + jnp.where(lane8 < 3, tile_c, 0.0)
    for q in range(KO):
        _, curv1, _ = steps[q]
        rz2 = value(2, q, 0)
        beta = rz2 / value(1, q, 0)
        curv = (
            value(2, q, 2) + value(2, q, 3) + 2.0 * beta * value(2, q, 1) + beta * beta * curv1
        )
        alpha = rz2 / curv
        for i, (vec, cur) in enumerate(((vec_r, cur_r), (vec_c, cur_c))):
            y = vec[3, q] + alpha * (cur[q] + beta * vec[4, q])
            if i == 0:
                fin_r[kb + q] = y
                y = pltpu.roll(y, 128 - RL, 1)
            else:
                col_out[kb + q] = y
            fin[i, q] = y
    swap = remote(fin, fin_x, pair_s.at[2], pair_r.at[2], sibling)
    swap.start()
    swap.wait()
    for q in range(KO):
        fin_r[ks + q] = fin_x[0, q]
        col_out[ks + q] = fin_x[1, q]

    @pl.loop(0, K)
    def _(k):
        y = fin_r[k]
        row_out[k] = y
        y = y + drow[k]
        c = col_out[k]
        for r in range(RL):
            rows = pl.ds(r * S, S)
            t = jnp.broadcast_to(y[:, r : r + 1], (S, IL)) + (c - grad[k, rows, :])
            cell[k, r] = (scal[k, rows, :] * t).astype(BF16)
        pltpu.make_async_copy(cell.at[k], cell_hbm.at[k], out_sem.at[k]).start()

    for k in range(K):
        pltpu.make_async_copy(cell.at[k], cell_hbm.at[k], out_sem.at[k]).wait()


def local(pos, low, high, upper, supp, att_r, att_c, drow, dcol):
    turned = jnp.pad(jnp.transpose(drow, (0, 2, 1)), ((0, 0), (0, 0), (0, 128 - RL)))
    V, DMA = pltpu.VMEM, pltpu.SemaphoreType.DMA
    cells = (K, RL, S, IL)
    scratch = [
        V(cells, BF16), V(cells, BF16), V(cells, BF16),
        V((RL, S, IL), jnp.int32), V((RL, S, IL), jnp.int32),
        V((K, S, 128), F32), V((K, S, IL), F32),
        DMA((3, K)), DMA((4,)),
        V((K, RL * S, IL), F32), V((KO, RL * S, IL), F32), V((K, RL * S, IL), F32),
        V((K, RL * S, IL), F32),
        V((RL, S, IL), F32), V((RL, S, IL), F32), V((RL, S, IL), F32),
        V((K, S, IL), jnp.int32),
        V((K, 4, S, 128), F32), V((KO, 4, S, 128), F32), DMA((3,)), DMA((3,)),
        V((KO, S, 2 * RL, 2 * IL), BF16), V((KO, S, IL, 256), BF16),
        V((96, 128), F32), V((NZ, 96, 128), F32),
        V((2, 64, 128), F32), V((2, 4, 64, 128), F32), V((2, 64, 128), F32), V((2, 4, 64, 128), F32),
        DMA((5,)), DMA((5,)),
        V((2, 48, 128), F32), V((2, NZ, 48, 128), F32), DMA((2,)), DMA((2,)),
        V((2, 2, 32, 128), F32), V((2, 2, 4, 32, 128), F32),
        V((2, 2, 32, 128), F32), V((2, 2, 4, 32, 128), F32),
        DMA((2, 4)), DMA((2, 4)),
        V((3, 8, 128), F32), V((3, NZ, 8, 128), F32), V((3, 8, 128), F32), V((3, NX * NY, 8, 128), F32),
        DMA((6,)), DMA((6,)),
        V((ROUNDS + 1, KO, S, 128), F32), V((ROUNDS + 1, KO, S, 128), F32),
        V((KO, S, 128), F32), V((KO, S, 128), F32), V((KO, S, 128), F32), V((KO, S, 128), F32),
        V((5, KO, S, 128), F32), V((5, KO, S, 128), F32),
        V((KO, S, 128), F32), V((KO, S, 128), F32),
        V((3, 8, 128), F32),
        V((2, KO, S, 128), F32), V((2, KO, S, 128), F32), V((K, S, 128), F32),
        V(cells, BF16), DMA((K,)),
    ]
    any_spec = pl.BlockSpec(memory_space=pl.ANY)
    smem_spec = pl.BlockSpec(memory_space=pltpu.SMEM)
    vmem_spec = pl.BlockSpec(memory_space=pltpu.VMEM)
    cell, row, col = pl.pallas_call(
        kernel,
        out_shape=(
            jax.ShapeDtypeStruct(cells, BF16),
            jax.ShapeDtypeStruct((K, S, 128), F32),
            jax.ShapeDtypeStruct((K, S, IL), F32),
        ),
        in_specs=[any_spec] * 5 + [smem_spec] * 2 + [any_spec] * 2,
        out_specs=(any_spec, vmem_spec, vmem_spec),
        scratch_shapes=scratch,
        compiler_params=pltpu.CompilerParams(
            collective_id=0, has_side_effects=True, vmem_limit_bytes=50 * 1024 * 1024
        ),
    )(pos, low, high, upper, supp, att_r, att_c, turned, dcol)
    return cell, jnp.transpose(row[:, :, :RL], (0, 2, 1)), col


def solution(mesh):
    cells = P(None, "region", None, "industry")
    return jax.shard_map(
        local,
        mesh=mesh,
        in_specs=(
            cells, cells, cells,
            P("region", None, "industry"), P("region", None, "industry"),
            P(), P(), P(None, "region", None), P(None, None, "industry"),
        ),
        out_specs=(cells, P(None, "region", None), P(None, None, "industry")),
        check_vma=False,
    )
```

time: 1710 us -> 132 us (0.08)
  waiting for transfers between devices: 948 us -> 0 us
  blocking collectives: 645 us -> 0 us
  Pallas kernels: 0 us -> 124 us
  other arithmetic: 99.3 us -> 0 us
    psum x10 -> x0, waiting for transfers between devices: 948 us -> none  [col_margin(): return lax.psum(partial_value, 'region')]
    psum x15 -> x0, blocking collectives: 645 us -> none  [the longest x5 375 us: inner_pair(): lax.psum(local_pair(first_row, second_row, first_col, second_col), ('regi...]
    pallas_call x0 -> x1, Pallas kernels: none -> 124 us  [local(): pl.pallas_call(kernel, out_shape=(jax.ShapeDtypeStruct(cells, BF16), jax....]
    reduce_sum x21 -> x0, other arithmetic: 53.3 us -> none  [the longest x6 18.8 us: couple(): left = row_margin(jnp.sum(scaling * part_col[:, None, :, :], axis=3))]
    div x17 -> x0, other arithmetic: 20.3 us -> none  [the longest x6 9.47 us: precondition(): base_row, base_col = (vec_row / diag_row, vec_col / diag_col)]
  transfers between devices with their start and end apart: 10 -> 0, of which waited for: 10 -> 0; matrix products, arithmetic and copies ran while one was open for 1% -> 0% of each run, Pallas kernels for 0% -> 0%
where the time goes in v1:
time: 132 us
  Pallas kernels  124 us (94%)
  local copies, waits for them, and re-layouts  7.39 us (6%)
    pallas_call x1, Pallas kernels, local(): pl.pallas_call(kernel, out_shape=(jax.ShapeDtypeStruct(cells, BF16), jax....  124 us
    unnamed x12, local copies, waits for them, and re-layouts  5.91 us

profile of v1, /device:TPU:1, one launch (start us, length us, event | category | flops | bytes accessed | tf_op | source)
XLA Modules:
  0.0 131.5 jit_solution(10352108729435601095)
XLA Ops:
  0.6 0.8 pad.4.drow_hbm
  1.5 0.0 copy-start
  1.5 1.0 copy-done
  2.5 0.0 copy-start.1
  2.5 1.0 copy-done.1
  3.5 0.0 copy-start.2
  3.5 0.8 copy-done.2
  4.3 0.0 copy-start.3
  4.3 0.7 copy-done.3
  5.0 0.0 copy-start.4
  5.0 0.7 copy-done.4
  5.6 123.5 %shard_map.112 = (bf16[8,48,16,128]{3,2,1,0:T(8,128)(2,1)S(1)}, f32[8,16,128]{2,1,0:T(8,128)S(1)}, f32[8,16,128]{2,1,0:T(8,128)S(1)}) custom-call(bf16[8,48,16,128]{3,2,1,0:T(8,128)(2,1)} %pos_hbm.1, bf16[8,48,16,128]{3,2,1,0:T(8,128)(2,1)} %low_hbm.1, bf16[8,48,16,128]{3,2,1,0:T(8,128)(2,1)} %high_hbm.1, s32[48,16,128]{2,1,0:T(8,128)S(1)} %copy-done, ...), custom_call_target="tpu_custom_call" | custom-call | tf_op jit(solution)/shard_map/pallas_call | solution.py:544
  129.1 0.6 slice_bitcast_fusion
  129.8 1.1 copy.14
  130.9 0.6 copy.15
Async XLA Ops:
  1.5 1.0 copy-start
  2.5 1.0 copy-start.1
  3.5 0.8 copy-start.2
  4.3 0.7 copy-start.3
  5.0 0.7 copy-start.4

commit v2 on v1

--- a/solution.py
+++ b/solution.py
@@ -154,11 +154,10 @@
         dc = dcol[k]
         ky = key[k]
 
-        def body(b, carry):
-            row_s, row_m, col_s, col_m = carry
-            for i in range(2):
-                r = b * 2 + i
-                rows = pl.ds(pl.multiple_of(r * S, S), S)
+        row_s, row_m, col_s, col_m = zero, zero, zero, zero
+        if True:
+            for r in range(RL):
+                rows = pl.ds(r * S, S)
                 p = pos[k, r].astype(F32)
                 dl = low[k, r].astype(F32)
                 du = high[k, r].astype(F32)
@@ -181,9 +180,6 @@
                 col_m = col_m + m
                 row_s = jnp.where(lane == r, jnp.sum(sc, axis=1, keepdims=True), row_s)
                 row_m = jnp.where(lane == r, jnp.sum(m, axis=1, keepdims=True), row_m)
-            return row_s, row_m, col_s, col_m
-
-        row_s, row_m, col_s, col_m = lax.fori_loop(0, RL // 2, body, (zero, zero, zero, zero))
         part[k, 0] = row_s
         part[k, 1] = row_m
         part[k, 2] = col_s
@@ -539,6 +535,7 @@
         V(cells, BF16), DMA((K,)),
     ]
     any_spec = pl.BlockSpec(memory_space=pl.ANY)
+    hbm_spec = pl.BlockSpec(memory_space=pltpu.HBM)
     smem_spec = pl.BlockSpec(memory_space=pltpu.SMEM)
     vmem_spec = pl.BlockSpec(memory_space=pltpu.VMEM)
     cell, row, col = pl.pallas_call(
@@ -548,7 +545,7 @@
             jax.ShapeDtypeStruct((K, S, 128), F32),
             jax.ShapeDtypeStruct((K, S, IL), F32),
         ),
-        in_specs=[any_spec] * 5 + [smem_spec] * 2 + [any_spec] * 2,
+        in_specs=[hbm_spec] * 5 + [smem_spec] * 2 + [hbm_spec] * 2,
         out_specs=(any_spec, vmem_spec, vmem_spec),
         scratch_shapes=scratch,
         compiler_params=pltpu.CompilerParams(

time: 132 us -> 115 us (0.87)
  Pallas kernels: 124 us -> 106 us
    pallas_call x1, Pallas kernels: 124 us -> 106 us  [local(): pl.pallas_call(kernel, out_shape=(jax.ShapeDtypeStruct(cells, BF16), jax....]
where the time goes in v2:
time: 115 us; the launch traced here: 114 us
  Pallas kernels  106 us (92%)
  local copies, waits for them, and re-layouts  7.39 us (6%)
    pallas_call x1, Pallas kernels, local(): pl.pallas_call(kernel, out_shape=(jax.ShapeDtypeStruct(cells, BF16), jax....  106 us
    unnamed x12, local copies, waits for them, and re-layouts  5.91 us

profile of v2, /device:TPU:1, one launch (start us, length us, event | category | flops | bytes accessed | tf_op | source)
XLA Modules:
  0.0 114.5 jit_solution(2485531773271319344)
XLA Ops:
  0.6 0.8 pad.4.drow_hbm
  1.5 0.0 copy-start
  1.5 1.0 copy-done
  2.5 0.0 copy-start.1
  2.5 1.0 copy-done.1
  3.5 0.0 copy-start.2
  3.5 0.8 copy-done.2
  4.3 0.0 copy-start.3
  4.3 0.7 copy-done.3
  5.0 0.0 copy-start.4
  5.0 0.7 copy-done.4
  5.6 106.4 %shard_map.112 = (bf16[8,48,16,128]{3,2,1,0:T(8,128)(2,1)S(1)}, f32[8,16,128]{2,1,0:T(8,128)S(1)}, f32[8,16,128]{2,1,0:T(8,128)S(1)}) custom-call(bf16[8,48,16,128]{3,2,1,0:T(8,128)(2,1)} %pos_hbm.1, bf16[8,48,16,128]{3,2,1,0:T(8,128)(2,1)} %low_hbm.1, bf16[8,48,16,128]{3,2,1,0:T(8,128)(2,1)} %high_hbm.1, s32[48,16,128]{2,1,0:T(8,128)S(1)} %copy-done, ...), custom_call_target="tpu_custom_call" | custom-call | tf_op jit(solution)/shard_map/pallas_call | solution.py:541
  112.1 0.6 slice_bitcast_fusion
  112.7 1.1 copy.14
  113.8 0.6 copy.15
Async XLA Ops:
  1.5 1.0 copy-start
  2.5 1.0 copy-start.1
  3.5 0.8 copy-start.2
  4.3 0.7 copy-start.3
  5.0 0.7 copy-start.4

commit v3 on v2

--- a/solution.py
+++ b/solution.py
@@ -12,6 +12,7 @@
 KO = 4
 NZ, NX, NY = 8, 4, 4
 ROUNDS = 8
+VL = 50
 WEIGHT_ATTACK, BARRIER, SHIFT = 8.0, 0.5, 1.0
 Z_STEPS = (4, 3, 5, 2, 6, 1, 7)
 LINE_STEPS = (2, 1, 3)
@@ -32,28 +33,24 @@
 
 
 def pack(rows):
-    tiles = [rows[q][8 * h : 8 * h + 8] for q in range(KO) for h in range(2)]
+    tiles = [x[8 * h : 8 * h + 8] for x in rows for h in range(2)]
     lane = lax.broadcasted_iota(jnp.int32, (8, 128), 1)
-    packed = []
-    for i in range(6):
-        spare = pltpu.roll(tiles[6 + i // 3], 96 - 32 * (i % 3), 1)
-        packed.append(jnp.where(lane < 96, tiles[i], spare))
+    packed = [
+        jnp.where(lane < 96, tiles[i], pltpu.roll(tiles[3], 96 - 32 * i, 1)) for i in range(3)
+    ]
     return jnp.concatenate(packed, axis=0)
 
 
 def unpack(packed):
     lane = lax.broadcasted_iota(jnp.int32, (8, 128), 1)
     zero = jnp.zeros((8, 128), F32)
-    m = [packed[8 * i : 8 * i + 8] for i in range(6)]
+    m = [packed[8 * i : 8 * i + 8] for i in range(3)]
     tiles = [jnp.where(lane < 96, x, zero) for x in m]
-    for g in range(2):
-        a = pltpu.roll(m[3 * g], 32, 1)
-        b = pltpu.roll(m[3 * g + 1], 64, 1)
-        c = pltpu.roll(m[3 * g + 2], 96, 1)
-        tiles.append(
-            jnp.where(lane < 32, a, jnp.where(lane < 64, b, jnp.where(lane < 96, c, zero)))
-        )
-    return [jnp.concatenate([tiles[2 * q], tiles[2 * q + 1]], axis=0) for q in range(KO)]
+    a, b, c = (pltpu.roll(m[i], 32 + 32 * i, 1) for i in range(3))
+    tiles.append(
+        jnp.where(lane < 32, a, jnp.where(lane < 64, b, jnp.where(lane < 96, c, zero)))
+    )
+    return [jnp.concatenate([tiles[2 * q], tiles[2 * q + 1]], axis=0) for q in range(2)]
 
 
 def kernel(
@@ -62,10 +59,10 @@
     pos, low, high, upper, supp, drow, dcol, in_sem, small_sem,
     scal, scal_x, grad, drow_b, umat, amat, hmat, key, part, part_x, pair_s, pair_r,
     mat_c, mat_r,
-    ini_zs, ini_zr, ini_c1, ini_c1r, ini_c2, ini_c2r, ini_s, ini_r,
+    ini_zs, ini_zr, ini_as, ini_ar, ini_c1, ini_c1r, ini_c2, ini_c2r, ini_s, ini_r,
     zs, zr, z_ss, z_rs,
     c1, c1r, c2, c2r, c_ss, c_rs,
-    dzs, dzr, dps, dpr, d_ss, d_rs,
+    dzs, dzr, dps, dpr, dfr, d_ss, d_rs,
     hist_r, hist_c, dia_r, dia_c, inv_r, inv_c, vec_r, vec_c, cur_r, cur_c, scl,
     fin, fin_x, fin_r, cell, out_sem,
 ):
@@ -90,7 +87,12 @@
         for g in (2, 1, 3, 0)
         if h or g
     ]
-    everyone = [sibling] + z_peers + p_peers
+    o_peers = [
+        {"region": (lax.rem(ix + h, NX) * NY + lax.rem(iy + g, NY)) * 2 + 1 - core}
+        for h in (2, 1, 3, 0)
+        for g in (2, 1, 3, 0)
+    ]
+    everyone = z_peers + p_peers + o_peers
 
     barrier = pltpu.get_barrier_semaphore()
     for peer in everyone:
@@ -136,8 +138,7 @@
         for r in range(RL):
             drow_b[k, pl.ds(r * S, S), :] = jnp.broadcast_to(d[:, r : r + 1], (S, IL))
 
-    @pl.loop(0, RL)
-    def _(r):
+    for r in range(RL):
         u = upper[r].astype(F32)
         umat[r] = u
         amat[r] = supp[r].astype(F32)
@@ -198,45 +199,55 @@
     for q in range(KO):
         for i in range(2):
             ini_c1[q // 2, pl.ds(((q % 2) * 2 + i) * S, S), :] = part[kb + q, 2 + i] + part_x[q, 2 + i]
-    packed_s, packed_m = pack(row_s), pack(row_m)
-    ini_zs[0:48, :] = packed_s
-    ini_zs[48:96, :] = packed_m
-
-    def line_start(src, dst, ss, rs, first_x):
-        for h in range(3):
-            for half in range(2):
-                along_x = (half == 0) == first_x
-                peer = (x_peers if along_x else y_peers)[h]
-                slot = ix if along_x else iy
-                remote(src.at[half], dst.at[half, slot], ss.at[half], rs.at[half], peer).start()
-
-    def line_finish(src, dst, ss, rs, first_x):
-        for half in range(2):
-            along_x = (half == 0) == first_x
-            slot = ix if along_x else iy
-            dst[half, slot] = src[half]
-        for half in range(2):
-            got = dst.at[half, pl.ds(0, 3)]
-            c = remote(got, got, ss.at[half], rs.at[half], x_peers[0])
-            c.wait_recv()
-            c.wait_send()
-        return [dst[half, 0] + dst[half, 1] + dst[half, 2] + dst[half, 3] for half in range(2)]
+    packed = [pack(v[2 * i : 2 * i + 2]) for v in (row_s, row_m) for i in range(2)]
+    for n in range(12):
+        ini_zs[n % 8, 8 * (n // 8) : 8 * (n // 8) + 8, :] = packed[n // 3][8 * (n % 3) : 8 * (n % 3) + 8]
+    for n in range(4, 8):
+        ini_zs[n, 8:16, :] = jnp.zeros((8, 128), F32)
+
+    def line_start(src, dst, ss, rs, first_x, half):
+        along_x = (half == 0) == first_x
+        slot = ix if along_x else iy
+        for peer in x_peers if along_x else y_peers:
+            remote(src.at[half], dst.at[half, slot], ss.at[half], rs.at[half], peer).start()
+
+    def line_finish(src, dst, ss, rs, first_x, half):
+        slot = ix if (half == 0) == first_x else iy
+        dst[half, slot] = src[half]
+        got = dst.at[half, pl.ds(0, 3)]
+        c = remote(got, got, ss.at[half], rs.at[half], x_peers[0])
+        c.wait_recv()
+        c.wait_send()
+        return (dst[half, 0] + dst[half, 1]) + (dst[half, 2] + dst[half, 3])
+
+    def tree(t):
+        while len(t) > 1:
+            t = [t[i] + t[i + 1] for i in range(0, len(t), 2)]
+        return t[0]
 
     def z_start(src, dst, ss, rs):
         for peer in z_peers:
             remote(src, dst.at[iz], ss, rs, peer).start()
 
-    def z_finish(src, dst, ss, rs):
-        dst[iz] = src[...]
+    def z_wait(dst, ss, rs):
         got = dst.at[pl.ds(0, NZ - 1)]
         c = remote(got, got, ss, rs, z_peers[0])
         c.wait_recv()
         c.wait_send()
-        t = [dst[i] for i in range(NZ)]
-        return ((t[0] + t[1]) + (t[2] + t[3])) + ((t[4] + t[5]) + (t[6] + t[7]))
-
-    z_start(ini_zs, ini_zr, ini_s.at[0], ini_r.at[0])
-    line_start(ini_c1, ini_c1r, ini_s.at[pl.ds(1, 2)], ini_r.at[pl.ds(1, 2)], True)
+
+    def z_finish(src, dst, ss, rs):
+        dst[iz] = src[...]
+        z_wait(dst, ss, rs)
+        return tree([dst[i] for i in range(NZ)])
+
+    for h, peer in zip(Z_STEPS, z_peers):
+        remote(
+            ini_zs.at[lax.rem(iz + h, NZ)], ini_zr.at[iz], ini_s.at[0], ini_r.at[0], peer
+        ).start()
+    line_1 = (ini_c1, ini_c1r, ini_s.at[pl.ds(1, 2)], ini_r.at[pl.ds(1, 2)], True)
+    line_2 = (ini_c2, ini_c2r, ini_s.at[pl.ds(3, 2)], ini_r.at[pl.ds(3, 2)], False)
+    for half in range(2):
+        line_start(*line_1, half)
 
     pair_scal.wait()
 
@@ -256,32 +267,41 @@
     HALF_BUILD = KO * S // 2
     pl.loop(0, HALF_BUILD)(build)
 
-    halves = line_finish(ini_c1, ini_c1r, ini_s.at[pl.ds(1, 2)], ini_r.at[pl.ds(1, 2)], True)
     for half in range(2):
-        ini_c2[half] = halves[half]
-    line_start(ini_c2, ini_c2r, ini_s.at[pl.ds(3, 2)], ini_r.at[pl.ds(3, 2)], False)
+        ini_c2[half] = line_finish(*line_1, half)
+        line_start(*line_2, half)
+    ini_zr[iz] = ini_zs[iz]
+    z_wait(ini_zr, ini_s.at[0], ini_r.at[0])
+    ini_as[...] = tree([ini_zr[i] for i in range(NZ)])
+    z_start(ini_as, ini_ar, ini_s.at[5], ini_r.at[5])
 
     pl.loop(HALF_BUILD, KO * S)(build)
 
-    total = z_finish(ini_zs, ini_zr, ini_s.at[0], ini_r.at[0])
+    for half in range(2):
+        total = line_finish(*line_2, half)
+        for i in range(2):
+            q = 2 * half + i
+            d = total[i * 2 * S : i * 2 * S + S] + SHIFT
+            m = total[i * 2 * S + S : i * 2 * S + 2 * S]
+            inv = 1.0 / d
+            dia_c[q] = d
+            inv_c[q] = inv
+            hist_c[0, q] = m * inv
+            cur_c[q] = m * inv
+    ini_ar[iz] = ini_as[...]
+    z_wait(ini_ar, ini_s.at[5], ini_r.at[5])
+    tiles = [ini_ar[n % 8, 8 * (n // 8) : 8 * (n // 8) + 8, :] for n in range(12)]
+    sums = []
+    for n in range(4):
+        sums += unpack(jnp.concatenate(tiles[3 * n : 3 * n + 3], axis=0))
     used = lane < 2 * RL
-    for q, (d, m) in enumerate(zip(unpack(total[0:48]), unpack(total[48:96]))):
-        d = d + SHIFT
+    for q in range(KO):
+        d = sums[q] + SHIFT
         inv = jnp.where(used, 1.0 / d, 0.0)
         dia_r[q] = d
         inv_r[q] = inv
-        hist_r[0, q] = m * inv
-        cur_r[q] = m * inv
-    halves = line_finish(ini_c2, ini_c2r, ini_s.at[pl.ds(3, 2)], ini_r.at[pl.ds(3, 2)], False)
-    for q in range(KO):
-        at = (q % 2) * 2 * S
-        d = halves[q // 2][at : at + S] + SHIFT
-        m = halves[q // 2][at + S : at + 2 * S]
-        inv = 1.0 / d
-        dia_c[q] = d
-        inv_c[q] = inv
-        hist_c[0, q] = m * inv
-        cur_c[q] = m * inv
+        hist_r[0, q] = sums[KO + q] * inv
+        cur_r[q] = sums[KO + q] * inv
 
     size_of = lax.rem(lax.broadcasted_iota(jnp.int32, (3 * S, 256), 0), S)
 
@@ -318,10 +338,7 @@
         c = remote(got, got, d_ss.at[n], d_rs.at[n], p_peers[0])
         c.wait_recv()
         c.wait_send()
-        t = [dpr[n, i] for i in range(NX * NY)]
-        while len(t) > 1:
-            t = [t[i] + t[i + 1] for i in range(0, len(t), 2)]
-        return t[0]
+        return tree([dpr[n, i] for i in range(NX * NY)])
 
     def zd_start(n, tile):
         dzs[n] = tile
@@ -333,29 +350,33 @@
     def value(n, q, d):
         return scl[n, q : q + 1, d : d + 1]
 
-    def first_step(hist, vec, cur):
-        for q in range(KO):
-            alpha = value(0, q, 0) / value(0, q, 1)
-            z0, w1, w3 = vec[0, q], hist[3, q], hist[5, q]
-            z1 = z0 - alpha * (z0 + w3)
-            vec[1, q] = z1
-            vec[2, q] = hist[0, q] - alpha * (z0 + w1)
-            vec[3, q] = alpha * z0
-            cur[q] = z1
-
-    def after_round(j, hist, vec, cur, dia, start):
+    def advance(j, hist, vec, cur, half):
+        mine = range(2 * half, 2 * half + 2)
+
         @pl.when((j != 2) & (j != 5))
         def _():
-            for q in range(KO):
+            for q in mine:
                 cur[q] = hist[j, q]
 
         @pl.when(j == 2)
         def _():
-            for q in range(KO):
+            for q in mine:
                 z0 = hist[0, q] - hist[1, q] + hist[2, q]
                 vec[0, q] = z0
                 cur[q] = z0
 
+        @pl.when(j == 5)
+        def _():
+            for q in mine:
+                alpha = value(0, q, 0) / value(0, q, 1)
+                z0, w1, w3 = vec[0, q], hist[3, q], hist[5, q]
+                z1 = z0 - alpha * (z0 + w3)
+                vec[1, q] = z1
+                vec[2, q] = hist[0, q] - alpha * (z0 + w1)
+                vec[3, q] = alpha * z0
+                cur[q] = z1
+
+    def send_dots(j, hist, vec, dia, start):
         @pl.when(j == 3)
         def _():
             rz, cv = [], []
@@ -389,47 +410,50 @@
                 (c2.at[n], c2r.at[n], c_ss.at[1, at], c_rs.at[1, at], False),
             )
 
+        def zed(n, half):
+            return zs.at[n, half], zr.at[n, half], z_ss.at[n, half], z_rs.at[n, half]
+
         @pl.when(j > 0)
         def _():
             first, second = lines(now)
-            halves = line_finish(*first)
             for half in range(2):
-                c2[now, half] = halves[half]
-            line_start(*second)
-            total = z_finish(zs.at[now], zr.at[now], z_ss.at[now], z_rs.at[now])
-            for q, t in enumerate(unpack(total)):
-                hist_r[j, q] = t * inv_r[q]
-
-            @pl.when(j == 5)
+                c2[now, half] = line_finish(*first, half)
+                line_start(*second, half)
+
+        @pl.when(j == 5)
+        def _():
+            scl[0] = zd_finish(0) + p_finish(0)
+
+        for half in range(2):
+
+            @pl.when(j > 0)
             def _():
-                scl[0] = zd_finish(0) + p_finish(0)
-                first_step(hist_r, vec_r, cur_r)
-
-            after_round(j, hist_r, vec_r, cur_r, dia_r, p_start)
-
-        @pl.when(j < ROUNDS)
-        def _():
-            for q in range(KO):
-                c1[nxt, q // 2, (q % 2) * S : (q % 2 + 1) * S, :] = couple_half(mat_c, cur_r[q], q, 96)
-            line_start(*lines(nxt)[0])
-
-        @pl.when(j > 0)
-        def _():
-            halves = line_finish(*lines(now)[1])
-            for q in range(KO):
-                at = (q % 2) * S
-                hist_c[j, q] = halves[q // 2][at : at + S] * inv_c[q]
-
-            @pl.when(j == 5)
+                for i, t in enumerate(unpack(z_finish(*zed(now, half)))):
+                    hist_r[j, 2 * half + i] = t * inv_r[2 * half + i]
+                advance(j, hist_r, vec_r, cur_r, half)
+
+            @pl.when(j < ROUNDS)
             def _():
-                first_step(hist_c, vec_c, cur_c)
-
-            after_round(j, hist_c, vec_c, cur_c, dia_c, zd_start)
-
-        @pl.when(j < ROUNDS)
-        def _():
-            zs[nxt] = pack([couple_half(mat_r, cur_c[q], q, 128) for q in range(KO)])
-            z_start(zs.at[nxt], zr.at[nxt], z_ss.at[nxt], z_rs.at[nxt])
+                for i in range(2):
+                    q = 2 * half + i
+                    c1[nxt, half, i * S : (i + 1) * S, :] = couple_half(mat_c, cur_r[q], q, 96)
+                line_start(*lines(nxt)[0], half)
+
+            @pl.when(j > 0)
+            def _():
+                total = line_finish(*lines(now)[1], half)
+                for i in range(2):
+                    hist_c[j, 2 * half + i] = total[i * S : (i + 1) * S] * inv_c[2 * half + i]
+                advance(j, hist_c, vec_c, cur_c, half)
+
+            @pl.when(j < ROUNDS)
+            def _():
+                mine = range(2 * half, 2 * half + 2)
+                zs[nxt, half] = pack([couple_half(mat_r, cur_c[q], q, 128) for q in mine])
+                z_start(*zed(nxt, half))
+
+        send_dots(j, hist_r, vec_r, dia_r, p_start)
+        send_dots(j, hist_c, vec_c, dia_c, zd_start)
 
     scl[1] = zd_finish(1) + p_finish(1)
     steps = []
@@ -459,32 +483,57 @@
     dots_r = second_step(hist_r, vec_r, cur_r, dia_r)
     cross = [2.0 * couple_half(mat_c, cur_r[q], q, 96) * cur_c[q] for q in range(KO)]
     zd_start(2, dot_tile(dots_c + [cross]))
-    tile_r = dot_tile(dots_r)
-    tile_c = zd_finish(2)
-    p_start(2, tile_r + jnp.where(lane8 == 3, tile_c, 0.0))
-    scl[2] = p_finish(2) + jnp.where(lane8 < 3, tile_c, 0.0)
-    for q in range(KO):
-        _, curv1, _ = steps[q]
-        rz2 = value(2, q, 0)
-        beta = rz2 / value(1, q, 0)
-        curv = (
-            value(2, q, 2) + value(2, q, 3) + 2.0 * beta * value(2, q, 1) + beta * beta * curv1
-        )
-        alpha = rz2 / curv
-        for i, (vec, cur) in enumerate(((vec_r, cur_r), (vec_c, cur_c))):
-            y = vec[3, q] + alpha * (cur[q] + beta * vec[4, q])
-            if i == 0:
-                fin_r[kb + q] = y
-                y = pltpu.roll(y, 128 - RL, 1)
-            else:
-                col_out[kb + q] = y
-            fin[i, q] = y
+
+    for i, (vec, cur) in enumerate(((vec_r, cur_r), (vec_c, cur_c))):
+        for q in range(KO):
+            for n, x in enumerate((vec[3, q], cur[q], vec[4, q])):
+                fin[i, n, q] = pltpu.roll(x, 128 - RL, 1) if i == 0 else x
     swap = remote(fin, fin_x, pair_s.at[2], pair_r.at[2], sibling)
     swap.start()
+
+    tile = dot_tile(dots_r)
+    for q in range(KO):
+        for d, x in ((11, value(1, q, 0)), (12, steps[q][1])):
+            tile = jnp.where((sub8 == q) & (lane8 == d), jnp.broadcast_to(x, (8, 128)), tile)
+    tile_c = zd_finish(2)
+    tile = tile + jnp.where(lane8 == 3, tile_c, 0.0)
+    tile = tile + pltpu.roll(jnp.where(lane8 < 3, tile_c, 0.0), 8, 1)
+    dps[2] = tile
+    chip = core * NX * NY + ix * NY + iy
+    for peer in o_peers + p_peers:
+        remote(dps.at[2], dfr.at[chip], d_ss.at[2], d_rs.at[2], peer).start()
+    dfr[chip] = tile
+    got = dfr.at[pl.ds(0, 2 * NX * NY - 1)]
+    c = remote(got, got, d_ss.at[2], d_rs.at[2], sibling)
+    c.wait_recv()
+    c.wait_send()
     swap.wait()
-    for q in range(KO):
-        fin_r[ks + q] = fin_x[0, q]
-        col_out[ks + q] = fin_x[1, q]
+    for owner in range(2):
+        own = owner == 0
+        who = core if own else 1 - core
+        base = kb if own else ks
+        total = tree([dfr[who * NX * NY + i] for i in range(NX * NY)])
+        same = dfr[who * NX * NY]
+        for q in range(KO):
+
+            def both(d):
+                return total[q : q + 1, d : d + 1] + same[q : q + 1, d + 8 : d + 9]
+
+            rz2 = both(0)
+            beta = rz2 / same[q : q + 1, 11:12]
+            curv = (
+                both(2) + total[q : q + 1, 3:4]
+                + 2.0 * beta * both(1) + beta * beta * same[q : q + 1, 12:13]
+            )
+            alpha = rz2 / curv
+            if own:
+                row = (vec_r[3, q], cur_r[q], vec_r[4, q])
+                col = (vec_c[3, q], cur_c[q], vec_c[4, q])
+            else:
+                row = (fin_x[0, 0, q], fin_x[0, 1, q], fin_x[0, 2, q])
+                col = (fin_x[1, 0, q], fin_x[1, 1, q], fin_x[1, 2, q])
+            fin_r[base + q] = row[0] + alpha * (row[1] + beta * row[2])
+            col_out[base + q] = col[0] + alpha * (col[1] + beta * col[2])
 
     @pl.loop(0, K)
     def _(k):
@@ -517,21 +566,22 @@
         V((K, S, IL), jnp.int32),
         V((K, 4, S, 128), F32), V((KO, 4, S, 128), F32), DMA((3,)), DMA((3,)),
         V((KO, S, 2 * RL, 2 * IL), BF16), V((KO, S, IL, 256), BF16),
-        V((96, 128), F32), V((NZ, 96, 128), F32),
+        V((NZ, 16, 128), F32), V((NZ, 16, 128), F32), V((16, 128), F32), V((NZ, 16, 128), F32),
         V((2, 64, 128), F32), V((2, 4, 64, 128), F32), V((2, 64, 128), F32), V((2, 4, 64, 128), F32),
-        DMA((5,)), DMA((5,)),
-        V((2, 48, 128), F32), V((2, NZ, 48, 128), F32), DMA((2,)), DMA((2,)),
+        DMA((6,)), DMA((6,)),
+        V((2, 2, 24, 128), F32), V((2, 2, NZ, 24, 128), F32), DMA((2, 2)), DMA((2, 2)),
         V((2, 2, 32, 128), F32), V((2, 2, 4, 32, 128), F32),
         V((2, 2, 32, 128), F32), V((2, 2, 4, 32, 128), F32),
         DMA((2, 4)), DMA((2, 4)),
         V((3, 8, 128), F32), V((3, NZ, 8, 128), F32), V((3, 8, 128), F32), V((3, NX * NY, 8, 128), F32),
+        V((2 * NX * NY, 8, 128), F32),
         DMA((6,)), DMA((6,)),
         V((ROUNDS + 1, KO, S, 128), F32), V((ROUNDS + 1, KO, S, 128), F32),
         V((KO, S, 128), F32), V((KO, S, 128), F32), V((KO, S, 128), F32), V((KO, S, 128), F32),
         V((5, KO, S, 128), F32), V((5, KO, S, 128), F32),
         V((KO, S, 128), F32), V((KO, S, 128), F32),
         V((3, 8, 128), F32),
-        V((2, KO, S, 128), F32), V((2, KO, S, 128), F32), V((K, S, 128), F32),
+        V((2, 3, KO, S, 128), F32), V((2, 3, KO, S, 128), F32), V((K, S, 128), F32),
         V(cells, BF16), DMA((K,)),
     ]
     any_spec = pl.BlockSpec(memory_space=pl.ANY)
@@ -549,7 +599,7 @@
         out_specs=(any_spec, vmem_spec, vmem_spec),
         scratch_shapes=scratch,
         compiler_params=pltpu.CompilerParams(
-            collective_id=0, has_side_effects=True, vmem_limit_bytes=50 * 1024 * 1024
+            collective_id=0, has_side_effects=True, vmem_limit_bytes=VL * 1024 * 1024
         ),
     )(pos, low, high, upper, supp, att_r, att_c, turned, dcol)
     return cell, jnp.transpose(row[:, :, :RL], (0, 2, 1)), col

time: 115 us -> 107 us (0.930)
  Pallas kernels: 106 us -> 98.3 us
    pallas_call x1, Pallas kernels: 106 us -> 98.3 us  [local(): pl.pallas_call(kernel, out_shape=(jax.ShapeDtypeStruct(cells, BF16), jax....]
where the time goes in v3:
time: 107 us; the launch traced here: 106 us
  Pallas kernels  98.3 us (92%)
  local copies, waits for them, and re-layouts  7.39 us (7%)
    pallas_call x1, Pallas kernels, local(): pl.pallas_call(kernel, out_shape=(jax.ShapeDtypeStruct(cells, BF16), jax....  98.3 us
    unnamed x12, local copies, waits for them, and re-layouts  5.91 us

profile of v3, /device:TPU:1, one launch (start us, length us, event | category | flops | bytes accessed | tf_op | source)
XLA Modules:
  0.0 106.3 jit_solution(9147167895055024497)
XLA Ops:
  0.6 0.8 pad.4.drow_hbm
  1.5 0.0 copy-start
  1.5 1.0 copy-done
  2.5 0.0 copy-start.1
  2.5 1.0 copy-done.1
  3.5 0.0 copy-start.2
  3.5 0.8 copy-done.2
  4.3 0.0 copy-start.3
  4.3 0.7 copy-done.3
  5.0 0.0 copy-start.4
  5.0 0.7 copy-done.4
  5.6 98.3 %shard_map.112 = (bf16[8,48,16,128]{3,2,1,0:T(8,128)(2,1)S(1)}, f32[8,16,128]{2,1,0:T(8,128)S(1)}, f32[8,16,128]{2,1,0:T(8,128)S(1)}) custom-call(bf16[8,48,16,128]{3,2,1,0:T(8,128)(2,1)} %pos_hbm.1, bf16[8,48,16,128]{3,2,1,0:T(8,128)(2,1)} %low_hbm.1, bf16[8,48,16,128]{3,2,1,0:T(8,128)(2,1)} %high_hbm.1, s32[48,16,128]{2,1,0:T(8,128)S(1)} %copy-done, ...), custom_call_target="tpu_custom_call" | custom-call | tf_op jit(solution)/shard_map/pallas_call | solution.py:591
  103.9 0.6 slice_bitcast_fusion
  104.6 1.1 %copy.14 = bf16[8,48,16,128]{3,2,1,0:T(8,128)(2,1)} copy(bf16[8,48,16,128]{3,2,1,0:T(8,128)(2,1)S(1)} %get-tuple-element.12) | data formatting | bytes 3145728
  105.7 0.6 copy.15
Async XLA Ops:
  1.5 1.0 copy-start
  2.5 1.0 copy-start.1
  3.5 0.8 copy-start.2
  4.3 0.7 copy-start.3
  5.0 0.7 copy-start.4
